TPU v7x, 32 devices: a whole 2x2x4 slice. The times are simulated.
32 devices in a mesh: scen: 8 (over z, x), row: 2 (over core), col: 2 (over y).
Axes of the slice: x: 2, y: 2, z: 4, core: 2. Of those that a mesh axis runs over, the one named last changes fastest.
Arguments:
- kkt: float32 [24, 768, 768], P('scen', ('row', 'col')), as said below
- border: float32 [24, 768, 4096], P('scen', None, ('row', 'col')), may hold values from -0.21875 to 0.21875
- first_diag: float32 [4096], P('scen'), may hold values from 0.5 to 1.5
- assignment: int32 [24], P('scen'), may hold values from 0 to 23, as said below
- panel: int32 [8], replicated, may hold values from 0 to 7, each once
Outputs:
- schur: float32 [4096, 4096], P('scen', ('row', 'col'))
- panel_factor: float32 [4096, 512], P('scen', ('row', 'col'))
Inputs may be any that keep to these rules, and one draw needn't show every extreme that they name: assignment is a permutation; with k = d * 3 + j (0 <= j < 3), assignment[k] is either k or (d XOR 1) * 3 + j, and the two scenarios of such a pair are either both fixed or swapped. panel is a permutation. Each kkt block is symmetric positive definite; after scaling by its diagonal, the off-diagonal part has spectral norm about one half.
All inputs are finite; a program needn't handle non-finite values.
Results may differ from a plain program's by a relative error of at most 0.00015.
Values sent between devices are 32-bit elements; how exact they have to be, the bound alone decides.
A program may use at most 192 MiB of HBM per device.

v0:
```python
import jax
import jax.numpy as jnp
from jax import lax
from jax.sharding import PartitionSpec as P

NK = 768
NF = 4096
PW = 512
NEWTON = 3
HIGH = lax.Precision.HIGHEST


def swapped(value, axis, distance):
    mask = 2**distance
    pairs = [(source, source ^ mask) for source in range(lax.axis_size(axis))]
    return lax.ppermute(value, axis, pairs)


def matmul(left, right):
    return jnp.dot(left, right, precision=HIGH, preferred_element_type=jnp.float32)


def contract(left, right):
    return lax.dot_general(
        left, right, (((0,), (0,)), ((), ())), precision=HIGH, preferred_element_type=jnp.float32
    )


def body(kkt, border, first_diag, assignment, panel):
    scen_index = lax.axis_index("scen")
    own_index = lax.axis_index(("row", "col"))
    slots = kkt.shape[0]
    partner = swapped(border, "scen", 0)
    kkt_all = lax.all_gather(kkt, ("row", "col"), axis=1, tiled=True)
    row_count = kkt.shape[1]
    col_count = border.shape[2]
    first_row = own_index * row_count
    row_ids = first_row + jnp.arange(row_count, dtype=jnp.int32)
    eye_rows = (jnp.arange(NK, dtype=jnp.int32)[None, :] == row_ids[:, None]).astype(jnp.float32)
    tile_total = jnp.zeros((NF, col_count), jnp.float32)
    for slot in range(slots):
        scenario_id = scen_index * slots + slot
        chosen = jnp.where(assignment[slot] == scenario_id, border[slot], partner[slot])
        kkt_rows = kkt[slot]
        kkt_full = kkt_all[slot]
        inv_diag = 1.0 / jnp.diagonal(kkt_full)
        local_inv = lax.dynamic_slice_in_dim(inv_diag, first_row, row_count)
        approx = (
            2.0 * (eye_rows * local_inv[:, None])
            - local_inv[:, None] * kkt_rows * inv_diag[None, :]
        )
        for step in range(NEWTON - 1):
            left = matmul(approx, kkt_full)

            def add_block(total, piece, start, left=left):
                return matmul(left, piece)

            product = add_block(
                jnp.zeros_like(approx),
                lax.all_gather(approx, ("row", "col"), axis=0, tiled=True),
                jnp.int32(0),
            )
            approx = 2.0 * approx - product

        def solve_piece(piece, start, chosen=chosen):
            return matmul(piece, chosen)

        solved = solve_piece(
            lax.all_gather(approx, ("row", "col"), axis=0, tiled=True), jnp.int32(0)
        )

        def border_piece(piece, start, solved=solved):
            return contract(piece, solved)

        tile = border_piece(
            lax.all_gather(chosen, ("row", "col"), axis=1, tiled=True), jnp.int32(0)
        )
        tile_total = tile_total + tile
    summed = lax.psum_scatter(tile_total, "scen", scatter_dimension=0, tiled=True)
    row_span = summed.shape[0]
    global_rows = scen_index * row_span + jnp.arange(row_span, dtype=jnp.int32)
    global_cols = own_index * col_count + jnp.arange(col_count, dtype=jnp.int32)
    on_diag = global_rows[:, None] == global_cols[None, :]
    schur = summed + jnp.where(on_diag, first_diag[:, None], 0.0)
    panel_start = panel[0] * PW
    panel_ids = panel_start + jnp.arange(PW, dtype=jnp.int32)
    select_cols = (global_cols[:, None] == panel_ids[None, :]).astype(jnp.float32)
    select_rows = (panel_ids[:, None] == global_rows[None, :]).astype(jnp.float32)
    panel_rows = lax.psum(matmul(schur, select_cols), ("row", "col"))
    block = lax.psum(matmul(select_rows, panel_rows), "scen")
    symmetric = 0.5 * (block + block.T)
    lower_factor = jnp.linalg.cholesky(symmetric)
    factor = lax.linalg.triangular_solve(
        lower_factor, panel_rows, left_side=False, lower=True, transpose_a=True
    )
    share = PW // lax.axis_size(("row", "col"))
    own_cols = lax.dynamic_slice_in_dim(factor, own_index * share, share, 1)
    return (schur, own_cols)


def solution(mesh):
    in_specs = (
        P("scen", ("row", "col"), None),
        P("scen", None, ("row", "col")),
        P("scen"),
        P("scen"),
        P(),
    )
    out_specs = (P("scen", ("row", "col")), P("scen", ("row", "col")))
    return jax.shard_map(body, mesh=mesh, in_specs=in_specs, out_specs=out_specs, check_vma=False)
```

profile of v0, /device:TPU:0, one launch (start us, length us, event | category | flops | bytes accessed | tf_op | source)
XLA Modules:
  0.0 1276.0 jit_solution(8011691956616219220)
XLA Ops:
  8.0 55.1 %all-gather.17.cloned.1.call-done = f32[3,768,768]{2,1,0:T(8,128)} async-done(((f32[3,192,768]{2,1,0:T(8,128)}), f32[3,768,768]{2,1,0:T(8,128)}) %all-gather.17.cloned.1.call-update) | async-done | bytes 7077904 | tf_op jit(solution)/shard_map/all_gather | solution.py:34
  68.8 12.2 gather_fusion.1
  81.0 12.1 gather_fusion.2
  107.7 19.3 %all-gather.31.cloned.1.call-done = f32[768,768]{1,0:T(8,128)} async-done(((f32[192,768]{1,0:T(8,128)}), f32[768,768]{1,0:T(8,128)}) %all-gather.31.cloned.1.call-update) | async-done | bytes 2359312 | tf_op jit(solution)/shard_map/all_gather | solution.py:60
  134.9 17.8 %all-gather.25.cloned.1.call-done = f32[768,768]{1,0:T(8,128)} async-done(((f32[192,768]{1,0:T(8,128)}), f32[768,768]{1,0:T(8,128)}) %all-gather.25.cloned.1.call-update) | async-done | bytes 2359312 | tf_op jit(solution)/shard_map/all_gather | solution.py:60
  160.7 17.4 %all-gather.19.cloned.1.call-done = f32[768,768]{1,0:T(8,128)} async-done(((f32[192,768]{1,0:T(8,128)}), f32[768,768]{1,0:T(8,128)}) %all-gather.19.cloned.1.call-update) | async-done | bytes 2359312 | tf_op jit(solution)/shard_map/all_gather | solution.py:60
  185.8 17.8 %all-gather.33.cloned.1.call-done = f32[768,768]{1,0:T(8,128)} async-done(((f32[192,768]{1,0:T(8,128)}), f32[768,768]{1,0:T(8,128)}) %all-gather.33.cloned.1.call-update) | async-done | bytes 2359312 | tf_op jit(solution)/shard_map/all_gather | solution.py:60
  212.9 16.2 %all-gather.27.cloned.1.call-done = f32[768,768]{1,0:T(8,128)} async-done(((f32[192,768]{1,0:T(8,128)}), f32[768,768]{1,0:T(8,128)}) %all-gather.27.cloned.1.call-update) | async-done | bytes 2359312 | tf_op jit(solution)/shard_map/all_gather | solution.py:60
  237.2 18.1 %all-gather.21.cloned.1.call-done = f32[768,768]{1,0:T(8,128)} async-done(((f32[192,768]{1,0:T(8,128)}), f32[768,768]{1,0:T(8,128)}) %all-gather.21.cloned.1.call-update) | async-done | bytes 2359312 | tf_op jit(solution)/shard_map/all_gather | solution.py:60
  262.2 151.2 %collective-permute-done = f32[3,768,1024]{2,1,0:T(8,128)} collective-permute-done((f32[3,768,1024]{2,1,0:T(8,128)}, f32[3,768,1024]{2,1,0:T(8,128)}, u32[]{:S(2)}, u32[]{:S(2)}) %collective-permute-start) | collective-permute-done | bytes 9437216 | tf_op jit(solution)/shard_map/ppermute | solution.py:16
  413.3 11.1 slice_select_fusion
  426.9 10.4 fusion.8
  437.3 12.2 fusion.10
  449.6 10.4 fusion.12
  460.0 46.7 %all-gather.39.cloned.1.call-done = f32[1,768,4096]{2,1,0:T(8,128)} async-done(((f32[1,768,1024]{2,1,0:T(8,128)}), f32[1,768,4096]{2,1,0:T(8,128)}) %all-gather.39.cloned.1.call-update) | async-done | bytes 12582928 | tf_op jit(solution)/shard_map/all_gather | solution.py:76
  506.7 45.4 %fusion.2 = f32[4096,1024]{1,0:T(8,128)} fusion(f32[768,1024]{1,0:T(8,128)} %fusion.10, f32[1,768,4096]{2,1,0:T(8,128)} %all-gather.39.cloned.1.call-done), kind=kOutput, calls=%fused_computation.8 | convolution fusion | flops 38654705664 | bytes 32505856 | tf_op jit(solution)/shard_map/dot_general | solution.py:24
  552.2 38.1 %all-gather.37.cloned.1.call-done = f32[1,768,4096]{2,1,0:T(8,128)} async-done(((f32[1,768,1024]{2,1,0:T(8,128)}), f32[1,768,4096]{2,1,0:T(8,128)}) %all-gather.37.cloned.1.call-update) | async-done | bytes 12582928 | tf_op jit(solution)/shard_map/all_gather | solution.py:76
  590.2 45.5 %fusion.4 = f32[4096,1024]{1,0:T(8,128)} fusion(f32[768,1024]{1,0:T(8,128)} %fusion.12, f32[1,768,4096]{2,1,0:T(8,128)} %all-gather.37.cloned.1.call-done), kind=kOutput, calls=%fused_computation.10 | convolution fusion | flops 38654705664 | bytes 32505856 | tf_op jit(solution)/shard_map/dot_general | solution.py:24
  635.8 38.1 %all-gather.41.cloned.1.call-done = f32[1,768,4096]{2,1,0:T(8,128)} async-done(((f32[1,768,1024]{2,1,0:T(8,128)}), f32[1,768,4096]{2,1,0:T(8,128)}) %all-gather.41.cloned.1.call-update) | async-done | bytes 12582928 | tf_op jit(solution)/shard_map/all_gather | solution.py:76
  673.9 47.5 %add_add_fusion = f32[4096,1024]{1,0:T(8,128)} fusion(f32[4096,1024]{1,0:T(8,128)} %fusion.4, f32[4096,1024]{1,0:T(8,128)} %fusion.2, f32[768,1024]{1,0:T(8,128)S(1)} %copy-done.3, f32[1,768,4096]{2,1,0:T(8,128)} %all-gather.41.cloned.1.call-done), kind=kOutput, calls=%fused_computation.5 | convolution fusion | flops 38663094272 | bytes 66060288 | tf_op jit(solution)/shard_map/dot_general | solution.py:24
  722.2 279.8 %reduce-scatter.2.cloned.1.call-done = f32[512,1024]{1,0:T(8,128)} async-done(((f32[4096,1024]{1,0:T(8,128)}), f32[512,1024]{1,0:T(8,128)}) %reduce-scatter.2.cloned.1.call-update) | async-done | bytes 2097168 | tf_op jit(solution)/shard_map/reduce_scatter | solution.py:79
  1008.4 35.3 %all-reduce.4.cloned.1.call-done = f32[512,512]{1,0:T(8,128)} async-done(((f32[512,512]{1,0:T(8,128)}), f32[512,512]{1,0:T(8,128)}) %all-reduce.4.cloned.1.call-update) | async-done | bytes 1048592 | tf_op jit(solution)/shard_map/psum | solution.py:89
  1047.1 78.9 %all-reduce.6.cloned.1.call-done = f32[512,512]{0,1:T(8,128)} async-done(((f32[512,512]{0,1:T(8,128)}), f32[512,512]{0,1:T(8,128)}) %all-reduce.6.cloned.1.call-update) | async-done | bytes 1048592 | tf_op jit(solution)/shard_map/psum | solution.py:90
  1128.5 11.7 cholesky.104
  1140.4 9.8 custom-call.30
  1150.9 11.9 cholesky.217
  1164.1 9.8 custom-call.31
  1174.6 11.7 cholesky.238
  1187.0 9.8 custom-call.32
  1197.5 11.9 cholesky.255
  1212.7 10.4 while.1
  1223.2 40.1 %custom-call.33 = f32[4,128,128]{1,2,0:T(8,128)S(1)} custom-call(f32[4,128,128]{2,1,0:T(8,128)} %get-tuple-element.9), custom_call_target="InvertDiagBlocksLowerTriangular" | custom-call | tf_op jit(solution)/shard_map/triangular_solve | solution.py:93
  (144 shorter events, 103.2 us)
Async XLA Ops:
  7.2 56.0 %all-gather.17.cloned.1.call-start = ((), (), s32[]{:S(2)}) async-start(), calls=%async_computation.1 | async-start | bytes 8847360 | tf_op jit(solution)/shard_map/all_gather | solution.py:34
  7.9 119.1 %all-gather.31.cloned.1.call-start = ((), (), s32[]{:S(2)}) async-start(), calls=%async_computation.8 | async-start | bytes 2949120 | tf_op jit(solution)/shard_map/all_gather | solution.py:60
  99.6 4.5 copy-start.2
  102.8 49.9 %all-gather.25.cloned.1.call-start = ((), (), s32[]{:S(2)}) async-start(), calls=%async_computation.5 | async-start | bytes 2949120 | tf_op jit(solution)/shard_map/all_gather | solution.py:60
  102.8 24.2 %copy-start.9 = (f32[192,768]{1,0:T(8,128)S(1)}, f32[192,768]{1,0:T(8,128)}, u32[]{:S(2)}) copy-start(f32[192,768]{1,0:T(8,128)} %get-tuple-element.30) | copy-start | bytes 1769476
  103.5 74.6 %all-gather.19.cloned.1.call-start = ((), (), s32[]{:S(2)}) async-start(), calls=%async_computation.2 | async-start | bytes 2949120 | tf_op jit(solution)/shard_map/all_gather | solution.py:60
  104.1 99.5 %all-gather.33.cloned.1.call-start = ((), (), s32[]{:S(2)}) async-start(), calls=%async_computation.9 | async-start | bytes 2949120 | tf_op jit(solution)/shard_map/all_gather | solution.py:60
  131.3 21.4 %copy-start.8 = (f32[192,768]{1,0:T(8,128)S(1)}, f32[192,768]{1,0:T(8,128)}, u32[]{:S(2)}) copy-start(f32[192,768]{1,0:T(8,128)} %get-tuple-element.32) | copy-start | bytes 1769476
  131.3 97.8 %all-gather.27.cloned.1.call-start = ((), (), s32[]{:S(2)}) async-start(), calls=%async_computation.6 | async-start | bytes 2949120 | tf_op jit(solution)/shard_map/all_gather | solution.py:60
  156.9 21.2 %copy-start.7 = (f32[192,768]{1,0:T(8,128)S(1)}, f32[192,768]{1,0:T(8,128)}, u32[]{:S(2)}) copy-start(f32[192,768]{1,0:T(8,128)} %get-tuple-element.31) | copy-start | bytes 1769476
  156.9 98.4 %all-gather.21.cloned.1.call-start = ((), (), s32[]{:S(2)}) async-start(), calls=%async_computation.3 | async-start | bytes 2949120 | tf_op jit(solution)/shard_map/all_gather | solution.py:60
  160.7 21.7 %copy-start.5 = (f32[192,768]{1,0:T(8,128)S(1)}, f32[192,768]{1,0:T(8,128)}, u32[]{:S(2)}) copy-start(f32[192,768]{1,0:T(8,128)} %convolution_subtract_fusion.1) | copy-start | bytes 1769476
  182.4 243.5 %all-gather.35.cloned.1.call-start = ((), (), s32[]{:S(2)}) async-start(), calls=%async_computation.10 | async-start | bytes 2949120 | tf_op jit(solution)/shard_map/all_gather | solution.py:69
  185.8 23.6 %copy-start.4 = (f32[192,768]{1,0:T(8,128)S(1)}, f32[192,768]{1,0:T(8,128)}, u32[]{:S(2)}) copy-start(f32[192,768]{1,0:T(8,128)} %convolution_subtract_fusion.3) | copy-start | bytes 1769476
  207.9 229.5 %all-gather.29.cloned.1.call-start = ((), (), s32[]{:S(2)}) async-start(), calls=%async_computation.7 | async-start | bytes 2949120 | tf_op jit(solution)/shard_map/all_gather | solution.py:69
  207.9 205.4 %collective-permute-start = (f32[3,768,1024]{2,1,0:T(8,128)}, f32[3,768,1024]{2,1,0:T(8,128)}, u32[]{:S(2)}, u32[]{:S(2)}) collective-permute-start(f32[3,768,1024]{2,1,0:T(8,128)} %param.6), channel_id=1, source_target_pairs={{0,4},{4,0},{8,12},{12,8},{16,20},{20,16},{24,28},{28,24},{1,5},{5... | collective-permute-start | bytes 28311560 | tf_op jit(solution)/shard_map/ppermute | solution.py:16
  212.9 20.9 %copy-start.6 = (f32[192,768]{1,0:T(8,128)S(1)}, f32[192,768]{1,0:T(8,128)}, u32[]{:S(2)}) copy-start(f32[192,768]{1,0:T(8,128)} %convolution_subtract_fusion.5) | copy-start | bytes 1769476
  233.3 216.2 %all-gather.23.cloned.1.call-start = ((), (), s32[]{:S(2)}) async-start(), calls=%async_computation.4 | async-start | bytes 2949120 | tf_op jit(solution)/shard_map/all_gather | solution.py:69
  237.2 22.4 %copy-start.13 = (s32[3]{0:T(128)S(1)}, s32[3]{0:T(128)}, u32[]{:S(2)}) copy-start(s32[3]{0:T(128)} %param.8) | copy-start | bytes 40
  259.6 247.2 %all-gather.39.cloned.1.call-start = ((), (), s32[]{:S(2)}) async-start(), calls=%async_computation.15 | async-start | bytes 15728640 | tf_op jit(solution)/shard_map/all_gather | solution.py:76
  424.5 165.8 %all-gather.37.cloned.1.call-start = ((), (), s32[]{:S(2)}) async-start(), calls=%async_computation.14 | async-start | bytes 15728640 | tf_op jit(solution)/shard_map/all_gather | solution.py:76
  425.1 1.9 copy-start
  425.1 248.8 %all-gather.41.cloned.1.call-start = ((), (), s32[]{:S(2)}) async-start(), calls=%async_computation.16 | async-start | bytes 15728640 | tf_op jit(solution)/shard_map/all_gather | solution.py:76
  425.8 576.1 %reduce-scatter.2.cloned.1.call-start = ((), (), s32[]{:S(2)}) async-start(), calls=%async_computation.11 | async-start | bytes 18874368 | tf_op jit(solution)/shard_map/reduce_scatter | solution.py:79
  437.3 12.2 copy-start.1
  552.2 121.8 %copy-start.3 = (f32[768,1024]{1,0:T(8,128)S(1)}, f32[768,1024]{1,0:T(8,128)}, u32[]{:S(2)}) copy-start(f32[768,1024]{1,0:T(8,128)} %fusion.8) | copy-start | bytes 9437188
  721.4 280.5 %copy-start.14 = (f32[512]{0:T(512)S(1)}, f32[512]{0:T(512)}, u32[]{:S(2)}) copy-start(f32[512]{0:T(512)} %param.7) | copy-start | bytes 6148
  721.5 322.2 %all-reduce.4.cloned.1.call-start = ((), (), s32[]{:S(2)}) async-start(), calls=%async_computation.12 | async-start | bytes 2097152 | tf_op jit(solution)/shard_map/psum | solution.py:89
  1003.8 1.3 copy-start.12
  1008.2 117.9 %all-reduce.6.cloned.1.call-start = ((), (), s32[]{:S(2)}) async-start(), calls=%async_computation.13 | async-start | bytes 2097152 | tf_op jit(solution)/shard_map/psum | solution.py:90
  1126.0 1.7 copy-start.10
  1174.2 89.1 %copy-start.11 = (f32[512,512]{1,0:T(8,128)S(1)}, f32[512,512]{1,0:T(8,128)}, u32[]{:S(2)}) copy-start(f32[512,512]{1,0:T(8,128)} %all-reduce.4.cloned.1.call-done) | copy-start | bytes 3145732
  (1 other events, 0.7 us)
Sparse Core Ops, SparseCore 0:
  9.5 53.5 all-gather.16
  102.9 24.0 all-gather.30
  128.5 24.0 all-gather.24
  154.1 23.9 all-gather.18
  179.5 24.0 all-gather.32
  205.0 24.0 all-gather.26
  231.2 24.0 all-gather.20
  256.9 24.0 all-gather.34
  282.5 24.0 all-gather.28
  308.6 24.0 all-gather.22
  424.6 82.0 all-gather.38
  508.1 82.0 all-gather.36
  591.8 82.0 all-gather.40
  721.6 280.2 reduce-scatter.1
  1008.3 35.3 all-reduce.3
  1047.2 78.7 all-reduce.5
where the time goes:
time: 1290 us; the launch traced here: 1280 us
  waiting for transfers between devices  833 us (65%)
  matrix products  231 us (18%)
  other arithmetic  136 us (11%)
  local copies, waits for them, and re-layouts  53.5 us (4%)
  between operations  19.3 us (1%)
    reduce_scatter x1, waiting for transfers between devices, body(): lax.psum_scatter(tile_total, 'scen', scatter_dimension=0, tiled=True)  280 us
    ppermute x1, waiting for transfers between devices, swapped(): return lax.ppermute(value, axis, pairs)  151 us
    dot_general x3, matrix products, contract(): lax.dot_general(left, right, (((0,), (0,)), ((), ())), precision=HIGH, pr...  138 us
    all_gather x3, waiting for transfers between devices, body(): lax.all_gather(chosen, ('row', 'col'), axis=1, tiled=True)  123 us
    all_gather x9, waiting for transfers between devices, body(): lax.all_gather(approx, ('row', 'col'), axis=0, tiled=True)  107 us
    dot_general x17, matrix products, matmul(): jnp.dot(left, right, precision=HIGH, preferred_element_type=jnp.float32)  85.6 us
    another operation x15, other arithmetic, body(): lower_factor = jnp.linalg.cholesky(symmetric)  79.5 us
    psum x1, waiting for transfers between devices, body(): block = lax.psum(matmul(select_rows, panel_rows), 'scen')  78.9 us
  transfers between devices with their start and end apart: 17, of which 14 were waited for; matrix products, arithmetic and copies ran while one was open for 14% of the time, Pallas kernels for 0%

commit v1 on v0

--- a/solution.py
+++ b/solution.py
@@ -2,6 +2,7 @@
 import jax.numpy as jnp
 from jax import lax
 from jax.sharding import PartitionSpec as P
+from jax.lax import all_to_all, axis_size
 
 NK = 768
 NF = 4096
@@ -73,7 +74,16 @@
             return contract(piece, solved)
 
         tile = border_piece(
-            lax.all_gather(chosen, ("row", "col"), axis=1, tiled=True), jnp.int32(0)
+            jnp.concatenate(
+                all_to_all(
+                    jnp.stack([chosen for _ in range(axis_size(("row", "col")))]),
+                    ("row", "col"),
+                    0,
+                    0,
+                ),
+                1,
+            ),
+            jnp.int32(0),
         )
         tile_total = tile_total + tile
     summed = lax.psum_scatter(tile_total, "scen", scatter_dimension=0, tiled=True)

time: 1290 us -> 1370 us (1.062)
  local copies, waits for them, and re-layouts: 53.5 us -> 84.3 us
  waiting for transfers between devices: 833 us -> 863 us
  starting transfers between devices: 2.97 us -> 23.8 us
    all_to_all x0 -> x3, waiting for transfers between devices: none -> 290 us  [body(): all_to_all(jnp.stack([chosen for _ in range(axis_size(('row', 'col')))]),...]
    all_gather x3 -> x0, waiting for transfers between devices: 123 us -> none  [body(): lax.all_gather(chosen, ('row', 'col'), axis=1, tiled=True)]
    all_gather x9, waiting for transfers between devices: 107 us -> 16.5 us  [body(): lax.all_gather(approx, ('row', 'col'), axis=0, tiled=True)]
    ppermute x1, waiting for transfers between devices: 151 us -> 108 us  [swapped(): return lax.ppermute(value, axis, pairs)]
    another operation x12 -> x18, local copies, waits for them, and re-layouts: 10.4 us -> 42.2 us  [the longest x6 31.7 us: body(): jnp.stack([chosen for _ in range(axis_size(('row', 'col')))])]
    all_to_all x0 -> x3, starting transfers between devices: none -> 19 us  [body(): all_to_all(jnp.stack([chosen for _ in range(axis_size(('row', 'col')))]),...]
  transfers between devices with their start and end apart: 17 -> 17, of which waited for: 14 -> 9; matrix products, arithmetic and copies ran while one was open for 14% -> 19% of each run, Pallas kernels for 0% -> 0%
where the time goes in v1:
time: 1370 us; the launch traced here: 1360 us
  waiting for transfers between devices  863 us (63%)
  matrix products  236 us (17%)
  other arithmetic  137 us (10%)
  local copies, waits for them, and re-layouts  84.3 us (6%)
  starting transfers between devices  23.8 us (2%)
  between operations  18.9 us (1%)
    all_to_all x3, waiting for transfers between devices, body(): all_to_all(jnp.stack([chosen for _ in range(axis_size(('row', 'col')))]),...  290 us
    reduce_scatter x1, waiting for transfers between devices, body(): lax.psum_scatter(tile_total, 'scen', scatter_dimension=0, tiled=True)  280 us
    dot_general x3, matrix products, contract(): lax.dot_general(left, right, (((0,), (0,)), ((), ())), precision=HIGH, pr...  137 us
    ppermute x1, waiting for transfers between devices, swapped(): return lax.ppermute(value, axis, pairs)  108 us
    dot_general x17, matrix products, matmul(): jnp.dot(left, right, precision=HIGH, preferred_element_type=jnp.float32)  92.3 us
    another operation x15, other arithmetic, body(): lower_factor = jnp.linalg.cholesky(symmetric)  79.7 us
    psum x1, waiting for transfers between devices, body(): block = lax.psum(matmul(select_rows, panel_rows), 'scen')  78.9 us
    all_gather x1, waiting for transfers between devices, body(): kkt_all = lax.all_gather(kkt, ('row', 'col'), axis=1, tiled=True)  52.1 us
  transfers between devices with their start and end apart: 17, of which 9 were waited for; matrix products, arithmetic and copies ran while one was open for 19% of the time, Pallas kernels for 0%

profile of v1, /device:TPU:0, one launch (start us, length us, event | category | flops | bytes accessed | tf_op | source)
XLA Modules:
  0.0 1363.0 jit_solution(4824254132349519217)
XLA Ops:
  11.0 52.1 %all-gather.11.cloned.1.call-done = f32[3,768,768]{2,1,0:T(8,128)} async-done(((f32[3,192,768]{2,1,0:T(8,128)}), f32[3,768,768]{2,1,0:T(8,128)}) %all-gather.11.cloned.1.call-update) | async-done | bytes 7077904 | tf_op jit(solution)/shard_map/all_gather | solution.py:35
  68.8 12.0 gather_fusion.1
  80.8 12.5 gather_fusion.2
  106.1 108.1 %collective-permute-done = f32[3,768,1024]{2,1,0:T(8,128)} collective-permute-done((f32[3,768,1024]{2,1,0:T(8,128)}, f32[3,768,1024]{2,1,0:T(8,128)}, u32[]{:S(2)}, u32[]{:S(2)}) %collective-permute-start) | collective-permute-done | bytes 9437216 | tf_op jit(solution)/shard_map/ppermute | solution.py:17
  214.2 10.3 fusion
  228.1 7.4 stack.30
  235.6 6.4 all-to-all-start.1
  262.8 142.5 %all-to-all-done.1 = f32[4,768,1024]{1,2,0:T(8,128)} async-done(((f32[4,768,1024]{1,2,0:T(8,128)}), f32[4,768,1024]{1,2,0:T(8,128)}, u32[]{:S(2)}, u32[]{:S(2)}) %all-to-all-start.1) | async-done | bytes 12582944 | tf_op jit(solution)/shard_map/all_to_all | solution.py:78
  405.3 7.4 stack.13
  412.7 6.3 all-to-all-start
  450.4 144.6 %all-to-all-done = f32[4,768,1024]{1,2,0:T(8,128)} async-done(((f32[4,768,1024]{1,2,0:T(8,128)}), f32[4,768,1024]{1,2,0:T(8,128)}, u32[]{:S(2)}, u32[]{:S(2)}) %all-to-all-start) | async-done | bytes 12582944 | tf_op jit(solution)/shard_map/all_to_all | solution.py:78
  595.0 7.4 stack.32
  602.4 6.3 all-to-all-start.2
  617.9 11.1 fusion.105
  629.0 11.3 fusion.103
  640.2 16.4 %all-gather.17.cloned.1.call-done = f32[768,768]{1,0:T(8,128)} async-done(((f32[192,768]{1,0:T(8,128)}), f32[768,768]{1,0:T(8,128)}) %all-gather.17.cloned.1.call-update) | async-done | bytes 2359312 | tf_op jit(solution)/shard_map/all_gather | solution.py:70
  656.7 9.6 fusion.101
  666.3 44.9 %fusion.104 = f32[4096,1024]{1,0:T(8,128)} fusion(f32[768,4096]{0,1:T(8,128)} %bitcast.10, f32[768,1024]{1,0:T(8,128)S(1)} %copy-done.2), kind=kOutput, calls=%fused_computation.174 | convolution fusion | flops 38654705664 | bytes 32505856 | tf_op jit(solution)/shard_map/dot_general | solution.py:25
  711.3 45.3 %fusion.102 = f32[4096,1024]{1,0:T(8,128)} fusion(f32[768,4096]{0,1:T(8,128)} %bitcast.3, f32[768,1024]{1,0:T(8,128)S(1)} %fusion.101), kind=kOutput, calls=%fused_computation.172 | convolution fusion | flops 38654705664 | bytes 32505856 | tf_op jit(solution)/shard_map/dot_general | solution.py:25
  759.4 47.3 %add_add_fusion = f32[4096,1024]{1,0:T(8,128)} fusion(f32[4096,1024]{1,0:T(8,128)} %fusion.102, f32[4096,1024]{1,0:T(8,128)} %fusion.104, f32[768,4096]{0,1:T(8,128)} %bitcast.17, f32[768,1024]{1,0:T(8,128)S(1)} %copy-done), kind=kOutput, calls=%fused_computation.5 | convolution fusion | flops 38663094272 | bytes 66060288 | tf_op jit(solution)/shard_map/dot_general | solution.py:25
  807.5 280.3 %reduce-scatter.2.cloned.1.call-done = f32[512,1024]{1,0:T(8,128)} async-done(((f32[4096,1024]{1,0:T(8,128)}), f32[512,1024]{1,0:T(8,128)}) %reduce-scatter.2.cloned.1.call-update) | async-done | bytes 2097168 | tf_op jit(solution)/shard_map/reduce_scatter | solution.py:89
  1094.2 35.3 %all-reduce.4.cloned.1.call-done = f32[512,512]{1,0:T(8,128)} async-done(((f32[512,512]{1,0:T(8,128)}), f32[512,512]{1,0:T(8,128)}) %all-reduce.4.cloned.1.call-update) | async-done | bytes 1048592 | tf_op jit(solution)/shard_map/psum | solution.py:99
  1132.9 78.9 %all-reduce.6.cloned.1.call-done = f32[512,512]{0,1:T(8,128)} async-done(((f32[512,512]{0,1:T(8,128)}), f32[512,512]{0,1:T(8,128)}) %all-reduce.6.cloned.1.call-update) | async-done | bytes 1048592 | tf_op jit(solution)/shard_map/psum | solution.py:100
  1215.5 11.7 cholesky.104
  1227.4 9.8 custom-call.30
  1237.8 12.1 cholesky.217
  1251.4 9.8 custom-call.31
  1261.8 11.7 cholesky.238
  1274.3 9.8 custom-call.32
  1284.7 11.9 cholesky.255
  1299.9 10.5 while.1
  1310.5 40.1 %custom-call.33 = f32[4,128,128]{1,2,0:T(8,128)S(1)} custom-call(f32[4,128,128]{2,1,0:T(8,128)} %get-tuple-element.9), custom_call_target="InvertDiagBlocksLowerTriangular" | custom-call | tf_op jit(solution)/shard_map/triangular_solve | solution.py:103
  (128 shorter events, 123.4 us)
Async XLA Ops:
  7.2 56.0 %all-gather.11.cloned.1.call-start = ((), (), s32[]{:S(2)}) async-start(), calls=%async_computation.4 | async-start | bytes 8847360 | tf_op jit(solution)/shard_map/all_gather | solution.py:35
  7.9 238.6 %all-gather.25.cloned.1.call-start = ((), (), s32[]{:S(2)}) async-start(), calls=%async_computation.11 | async-start | bytes 2949120 | tf_op jit(solution)/shard_map/all_gather | solution.py:61
  7.9 206.3 %collective-permute-start = (f32[3,768,1024]{2,1,0:T(8,128)}, f32[3,768,1024]{2,1,0:T(8,128)}, u32[]{:S(2)}, u32[]{:S(2)}) collective-permute-start(f32[3,768,1024]{2,1,0:T(8,128)} %param.6), channel_id=1, source_target_pairs={{0,4},{4,0},{8,12},{12,8},{16,20},{20,16},{24,28},{28,24},{1,5},{5... | collective-permute-start | bytes 28311560 | tf_op jit(solution)/shard_map/ppermute | solution.py:17
  99.8 3.8 copy-start.4
  102.8 153.1 %all-gather.19.cloned.1.call-start = ((), (), s32[]{:S(2)}) async-start(), calls=%async_computation.8 | async-start | bytes 2949120 | tf_op jit(solution)/shard_map/all_gather | solution.py:61
  103.6 320.0 %all-gather.13.cloned.1.call-start = ((), (), s32[]{:S(2)}) async-start(), calls=%async_computation.5 | async-start | bytes 2949120 | tf_op jit(solution)/shard_map/all_gather | solution.py:61
  235.6 169.8 %all-to-all-start.1 = ((f32[4,768,1024]{1,2,0:T(8,128)}), f32[4,768,1024]{1,2,0:T(8,128)}, u32[]{:S(2)}, u32[]{:S(2)}) async-start(f32[4,768,1024]{1,2,0:T(8,128)} %stack.30), calls=%async_computation.1 | async-start | bytes 25165824 | tf_op jit(solution)/shard_map/all_to_all | solution.py:78
  241.9 191.1 %all-gather.27.cloned.1.call-start = ((), (), s32[]{:S(2)}) async-start(), calls=%async_computation.12 | async-start | bytes 2949120 | tf_op jit(solution)/shard_map/all_gather | solution.py:61
  251.1 191.2 %all-gather.21.cloned.1.call-start = ((), (), s32[]{:S(2)}) async-start(), calls=%async_computation.9 | async-start | bytes 2949120 | tf_op jit(solution)/shard_map/all_gather | solution.py:61
  412.7 182.3 %all-to-all-start = ((f32[4,768,1024]{1,2,0:T(8,128)}), f32[4,768,1024]{1,2,0:T(8,128)}, u32[]{:S(2)}, u32[]{:S(2)}) async-start(f32[4,768,1024]{1,2,0:T(8,128)} %stack.13), calls=%async_computation | async-start | bytes 25165824 | tf_op jit(solution)/shard_map/all_to_all | solution.py:78
  419.0 194.3 %all-gather.15.cloned.1.call-start = ((), (), s32[]{:S(2)}) async-start(), calls=%async_computation.6 | async-start | bytes 2949120 | tf_op jit(solution)/shard_map/all_gather | solution.py:61
  428.1 189.8 %all-gather.29.cloned.1.call-start = ((), (), s32[]{:S(2)}) async-start(), calls=%async_computation.13 | async-start | bytes 2949120 | tf_op jit(solution)/shard_map/all_gather | solution.py:70
  437.6 191.4 %all-gather.23.cloned.1.call-start = ((), (), s32[]{:S(2)}) async-start(), calls=%async_computation.10 | async-start | bytes 2949120 | tf_op jit(solution)/shard_map/all_gather | solution.py:70
  602.4 157.1 %all-to-all-start.2 = ((f32[4,768,1024]{1,2,0:T(8,128)}), f32[4,768,1024]{1,2,0:T(8,128)}, u32[]{:S(2)}, u32[]{:S(2)}) async-start(f32[4,768,1024]{1,2,0:T(8,128)} %stack.32), calls=%async_computation.2 | async-start | bytes 25165824 | tf_op jit(solution)/shard_map/all_to_all | solution.py:78
  608.7 48.0 %all-gather.17.cloned.1.call-start = ((), (), s32[]{:S(2)}) async-start(), calls=%async_computation.7 | async-start | bytes 2949120 | tf_op jit(solution)/shard_map/all_gather | solution.py:70
  617.8 469.9 %reduce-scatter.2.cloned.1.call-start = ((), (), s32[]{:S(2)}) async-start(), calls=%async_computation.14 | async-start | bytes 18874368 | tf_op jit(solution)/shard_map/reduce_scatter | solution.py:89
  656.7 9.7 copy-start.2
  711.3 48.1 %copy-start = (f32[768,1024]{1,0:T(8,128)S(1)}, f32[768,1024]{1,0:T(8,128)}, u32[]{:S(2)}) copy-start(f32[768,1024]{1,0:T(8,128)} %fusion.105) | copy-start | bytes 9437188
  806.7 0.7 copy-start.6
  806.7 281.0 %copy-start.5 = (f32[512]{0:T(512)S(1)}, f32[512]{0:T(512)}, u32[]{:S(2)}) copy-start(f32[512]{0:T(512)} %param.7) | copy-start | bytes 6148
  806.8 322.7 %all-reduce.4.cloned.1.call-start = ((), (), s32[]{:S(2)}) async-start(), calls=%async_computation.15 | async-start | bytes 2097152 | tf_op jit(solution)/shard_map/psum | solution.py:99
  1089.6 1.3 copy-start.3
  1094.0 117.9 %all-reduce.6.cloned.1.call-start = ((), (), s32[]{:S(2)}) async-start(), calls=%async_computation.16 | async-start | bytes 2097152 | tf_op jit(solution)/shard_map/psum | solution.py:100
  1237.2 113.4 %copy-start.1 = (f32[512,512]{1,0:T(8,128)S(1)}, f32[512,512]{1,0:T(8,128)}, u32[]{:S(2)}) copy-start(f32[512,512]{1,0:T(8,128)} %all-reduce.4.cloned.1.call-done) | copy-start | bytes 3145732
Sparse Core Ops, SparseCore 0:
  9.5 53.5 all-gather.10
  102.9 24.0 all-gather.24
  128.6 24.0 all-gather.18
  154.1 24.0 all-gather.12
  251.2 38.6 all-gather.26
  291.3 36.8 all-gather.20
  428.2 38.6 all-gather.14
  468.5 36.7 all-gather.28
  506.9 36.7 all-gather.22
  618.0 38.6 all-gather.16
  806.9 280.8 reduce-scatter.1
  1094.1 35.3 all-reduce.3
  1133.0 78.7 all-reduce.5
